TPU v7x, 32 devices: a whole 2x2x4 slice. The times are simulated.
32 devices in a mesh: leaf: 8 (over z, core), sub: 4 (over y, x).
Axes of the slice: x: 2, y: 2, z: 4, core: 2. Of those that a mesh axis runs over, the one named last changes fastest.
Arguments:
- leaf_maps: float32 [32, 256, 1024], P('leaf', 'sub'), may hold values from -8 to 28, as said below
- order_one: int32 [8, 4], replicated, may hold values from 0 to 3, each once within a row
- order_two: int32 [4, 6], replicated, may hold values from 0 to 5, each once within a row
- top_data: float32 [16, 256, 256], P('leaf', 'sub'), may hold values from -6 to 6
Outputs:
- top_map: float32 [16, 256, 2048], P('leaf', 'sub')
- leaf_data: float32 [32, 256, 256], P('leaf', 'sub')
Inputs may be any that keep to these rules, and one draw needn't show every extreme that they name: Each leaf's block of 1024 rows of leaf_maps, read as a 1024 by 1024 matrix, is symmetric and positive definite.
All inputs are finite; a program needn't handle non-finite values. Where the computation divides by a largest or mean magnitude, that divisor is 1e-20 or more.
Results may differ from a plain program's by a relative error of at most 0.0001.
Values sent between devices are 32-bit elements; how exact they have to be, the bound alone decides.
No kernel may reach another device: no remote copies, remote signals or barrier semaphores. Data moves between devices by JAX's collectives and lax.ppermute only.
A program may use at most 64 MiB of HBM per device.

v0:
```python
import jax
import jax.numpy as jnp
from jax import lax
from jax.sharding import PartitionSpec as P

W = 256
K = 256
NS_STEPS = 4


def swapped(value, axis, apart):
    mask = 2**apart
    pairs = [(source, source ^ mask) for source in range(lax.axis_size(axis))]
    return lax.ppermute(value, axis, pairs)


def exact_dot(left_matrix, right_matrix):
    return jnp.dot(
        left_matrix,
        right_matrix,
        precision=lax.Precision.HIGHEST,
        preferred_element_type=jnp.float32,
    )


def interface_inverse(block_rows):
    slot_count, width_local, block_size = block_rows.shape
    full_block = lax.all_gather(block_rows, "sub", axis=1, tiled=True).reshape(
        block_size, block_size
    )
    row_bound = jnp.max(jnp.sum(jnp.abs(full_block), axis=1))
    iterate = jnp.eye(block_size, dtype=jnp.float32) / row_bound
    for iteration in range(NS_STEPS):
        iterate = 2.0 * iterate - exact_dot(exact_dot(full_block, iterate), iterate)
    return iterate


def shards(leaf_maps, order_one, order_two, top_data):
    width_local = leaf_maps.shape[1]
    group_index = lax.axis_index("leaf")
    member_index = lax.axis_index("sub")
    parity = group_index % 2
    is_first = parity == 0
    own_order = order_one[group_index]
    permuted = jnp.take(leaf_maps, own_order, axis=0)
    permuted = jnp.take(permuted.reshape(4, width_local, 4, W), own_order, axis=2).reshape(
        4, width_local, 4 * W
    )
    near_rows = permuted[:3]
    inner_piece = permuted[3]
    other_piece = swapped(inner_piece, "leaf", 0)
    first_piece = jnp.where(is_first, inner_piece, other_piece)
    second_piece = jnp.where(is_first, other_piece, inner_piece)
    block_one = first_piece[:, 3 * W :] + second_piece[:, 3 * W :]
    inverse_one = interface_inverse(block_one[None])
    coupling_one = near_rows[:, :, 3 * W :].reshape(3 * width_local, W)
    scaled_one = exact_dot(coupling_one, inverse_one)
    pieces = (
        lax.all_gather(first_piece[:, : 3 * W], "sub", axis=0, tiled=True),
        lax.all_gather(second_piece[:, : 3 * W], "sub", axis=0, tiled=True),
    )
    piece_rows = pieces[0].shape[0]
    joined = jnp.concatenate([pieces[0], pieces[1]], axis=1)
    coeff_part = scaled_one
    running_sum = exact_dot(coeff_part, joined)
    own_part = jnp.where(is_first, pieces[0], pieces[1]).reshape(piece_rows, 3, W)
    own_part = lax.dynamic_slice_in_dim(own_part, member_index * width_local, width_local, 2)
    kept_columns = own_part.reshape(piece_rows, 3 * width_local)
    product_one = running_sum
    right_one = kept_columns
    own_outer = near_rows[:, :, : 3 * W].reshape(3 * width_local, 3 * W)
    zero_one = jnp.zeros_like(own_outer)
    diagonal_one = jnp.where(
        is_first,
        jnp.concatenate([own_outer, zero_one], axis=1),
        jnp.concatenate([zero_one, own_outer], axis=1),
    )
    merged_one = (diagonal_one - product_one).reshape(3, width_local, 6 * W)
    node_index = group_index // 2
    node_first = node_index % 2 == 0
    node_order = order_two[node_index]
    node_rows = jnp.take(merged_one.reshape(3, width_local, 6, W), node_order, axis=2).reshape(
        3, width_local, 6 * W
    )
    position_table = jnp.sum(
        jnp.arange(6)[:, None] * (node_order[:, None] == jnp.arange(6)[None, :]).astype(jnp.int32),
        axis=0,
    )
    my_positions = jnp.take(position_table, 3 * parity + jnp.arange(3))
    slot_edges = node_order[4:6]
    slot_held = (slot_edges // 3 == parity).astype(jnp.float32)
    slot_piece = jnp.take(node_rows, slot_edges % 3, axis=0) * slot_held[:, None, None]
    node_piece = slot_piece + swapped(slot_piece, "leaf", 0)
    cousin_piece = swapped(node_piece, "leaf", 1)
    first_node = jnp.where(node_first, node_piece, cousin_piece)
    second_node = jnp.where(node_first, cousin_piece, node_piece)
    block_two = first_node[:, :, 4 * W :] + second_node[:, :, 4 * W :]
    inverse_two = interface_inverse(block_two)
    coupling_two = node_rows[:, :, 4 * W :].reshape(3 * width_local, 2 * W)
    scaled_two = exact_dot(coupling_two, inverse_two).reshape(3 * width_local, 2, W)
    top_first = 2 * (group_index % 4)
    pieces = (
        lax.all_gather(first_node[:, :, : 4 * W], "sub", axis=1, tiled=True),
        lax.all_gather(second_node[:, :, : 4 * W], "sub", axis=1, tiled=True),
    )
    piece_rows = pieces[0].shape[1]
    joined = jnp.concatenate([pieces[0], pieces[1]], axis=2)
    coeff_part = scaled_two.reshape(3 * width_local, 2 * piece_rows)
    running_sum = exact_dot(coeff_part, joined.reshape(2 * piece_rows, 8 * W))
    own_part = lax.dynamic_slice_in_dim(joined.reshape(2, piece_rows, 8, W), top_first, 2, 2)
    own_part = lax.dynamic_slice_in_dim(own_part, member_index * width_local, width_local, 3)
    kept_columns = own_part
    node_outer = node_rows[:, :, : 4 * W].reshape(3 * width_local, 4 * W)
    zero_two = jnp.zeros_like(node_outer)
    diagonal_two = jnp.where(
        node_first,
        jnp.concatenate([node_outer, zero_two], axis=1),
        jnp.concatenate([zero_two, node_outer], axis=1),
    )
    top_rows = (diagonal_two - running_sum).reshape(3, width_local, 8 * W)
    node_offset = 4 * (node_index % 2)
    buffer = jnp.zeros((8, width_local, 8 * W), jnp.float32)
    for row_slot in range(3):
        target = node_offset + my_positions[row_slot]
        marker = ((jnp.arange(8) == target) & (my_positions[row_slot] < 4)).astype(jnp.float32)
        buffer = buffer + marker[:, None, None] * top_rows[row_slot][None]
    upper_half = node_index % 2
    outgoing = lax.dynamic_slice_in_dim(buffer, 4 * (1 - upper_half), 4, 0)
    retained = lax.dynamic_slice_in_dim(buffer, 4 * upper_half, 4, 0)
    retained = retained + swapped(outgoing, "leaf", 1)
    outgoing_near = lax.dynamic_slice_in_dim(retained, 2 * (1 - parity), 2, 0)
    own_part = lax.dynamic_slice_in_dim(retained, 2 * parity, 2, 0)
    top_map = own_part + swapped(outgoing_near, "leaf", 0)
    partial_two = exact_dot(
        kept_columns.reshape(2 * W, 2 * width_local), top_data.reshape(2 * width_local, K)
    )
    partial_two = lax.psum(partial_two, "sub")
    spread = lax.dynamic_update_slice_in_dim(
        jnp.zeros((8, width_local, K), jnp.float32), top_data, top_first, 0
    )
    for bit_index in range(2):
        other_sum, other_spread = swapped((partial_two, spread), "leaf", bit_index)
        partial_two = partial_two + other_sum
        spread = spread + other_spread
    inner_two = -exact_dot(inverse_two, partial_two)
    inner_local = lax.dynamic_slice_in_dim(
        inner_two.reshape(2, W, K), member_index * width_local, width_local, 1
    )
    candidates = jnp.concatenate(
        [lax.dynamic_slice_in_dim(spread, node_offset, 4, 0), inner_local], axis=0
    )
    node_data = jnp.take(candidates, my_positions, axis=0)
    partial_one = exact_dot(right_one, node_data.reshape(3 * width_local, K))
    partial_one = lax.psum(partial_one, "sub")
    partial_one = partial_one + swapped(partial_one, "leaf", 0)
    inner_one = -exact_dot(inverse_one, partial_one)
    inner_slice = lax.dynamic_slice_in_dim(inner_one, member_index * width_local, width_local, 0)
    permuted_data = jnp.concatenate([node_data, inner_slice[None]], axis=0)
    restore = (own_order[:, None] == jnp.arange(4)[None, :]).astype(jnp.float32)
    leaf_data = jnp.zeros((4, width_local, K), jnp.float32)
    for position in range(4):
        leaf_data = leaf_data + restore[position][:, None, None] * permuted_data[position][None]
    return (top_map, leaf_data)


def solution(mesh):
    in_specs = (P("leaf", "sub", None), P(), P(), P("leaf", "sub", None))
    out_specs = (P("leaf", "sub", None), P("leaf", "sub", None))
    return jax.shard_map(shards, mesh=mesh, in_specs=in_specs, out_specs=out_specs, check_vma=False)
```

profile of v0, /device:TPU:0, one launch (start us, length us, event | category | flops | bytes accessed | tf_op | source)
XLA Modules:
  0.0 383.9 jit_solution(1197257132475756715)
XLA Ops:
  13.0 10.0 %all-gather = f32[256,256]{1,0:T(8,128)S(1)} all-gather(f32[64,256]{1,0:T(8,128)S(1)} %slice_add_fusion.1), channel_id=2, replica_groups=mesh['leaf'=8,'sub'=4] {'sub'}, dimensions={0}, use_global_device_ids=true | all-gather | bytes 327680 | tf_op jit(solution)/shard_map/all_gather | solution.py:28
  27.6 12.5 %all_gather.20 = f32[256,768]{1,0:T(8,128)S(1)} all-gather(f32[64,768]{1,0:T(8,128)S(1)} %slice.143), channel_id=1, replica_groups=mesh['leaf'=8,'sub'=4] {'sub'}, dimensions={0}, use_global_device_ids=true | all-gather | bytes 983040 | tf_op jit(solution)/shard_map/all_gather | solution.py:60
  40.0 10.2 %all_gather.19 = f32[256,768]{1,0:T(8,128)S(1)} all-gather(f32[64,768]{1,0:T(8,128)S(1)} %slice.142), channel_id=1, replica_groups=mesh['leaf'=8,'sub'=4] {'sub'}, dimensions={0}, use_global_device_ids=true | all-gather | bytes 983040 | tf_op jit(solution)/shard_map/all_gather | solution.py:59
  50.6 1.2 convolution_subtract_fusion
  51.8 1.5 reshape_reshape.3
  53.3 2.8 copy.20
  56.1 1.9 gather_fusion.3
  59.1 2.3 collective-permute-done.1
  61.4 1.0 fusion.90
  62.4 1.6 collective-permute-start.2
  64.0 18.3 %collective-permute-done.2 = f32[2,64,1536]{2,1,0:T(8,128)} collective-permute-done((f32[2,64,1536]{2,1,0:T(8,128)}, f32[2,64,1536]{2,1,0:T(8,128)}, u32[]{:S(2)}, u32[]{:S(2)}) %collective-permute-start.2) | collective-permute-done | bytes 786464 | tf_op jit(solution)/shard_map/ppermute | solution.py:14
  82.3 1.5 broadcast_select_fusion.3
  85.5 1.9 slice.148
  95.5 16.9 %all-gather.5.cloned.1.call-done = f32[2,256,512]{2,1,0:T(8,128)} async-done(((f32[2,64,512]{2,1,0:T(8,128)}), f32[2,256,512]{2,1,0:T(8,128)}) %all-gather.5.cloned.1.call-update) | async-done | bytes 1048592 | tf_op jit(solution)/shard_map/all_gather | solution.py:28
  112.4 1.4 abs_reduce_fusion
  115.1 3.1 fusion.2
  118.2 1.8 fusion.7
  120.0 1.8 fusion.45
  121.8 1.8 convolution_subtract_fusion.4
  123.7 1.8 fusion.46
  125.6 1.8 convolution_subtract_fusion.3
  127.4 2.1 fusion.47
  129.5 1.9 convolution_subtract_fusion.2
  132.3 17.2 %all-gather.7.cloned.1.call-done = f32[2,256,1024]{2,1,0:T(8,128)} async-done(((f32[2,64,1024]{2,1,0:T(8,128)}), f32[2,256,1024]{2,1,0:T(8,128)}) %all-gather.7.cloned.1.call-update) | async-done | bytes 2097168 | tf_op jit(solution)/shard_map/all_gather | solution.py:103
  149.5 3.2 constant_dynamic-update-slice_fusion.1
  152.7 34.4 %all-gather.9.cloned.1.call-done = f32[2,256,1024]{2,1,0:T(8,128)} async-done(((f32[2,64,1024]{2,1,0:T(8,128)}), f32[2,256,1024]{2,1,0:T(8,128)}) %all-gather.9.cloned.1.call-update) | async-done | bytes 2097168 | tf_op jit(solution)/shard_map/all_gather | solution.py:104
  187.1 3.2 constant_dynamic-update-slice_fusion
  190.3 7.3 %copy.24 = f32[2,256,2048]{1,0,2:T(2,128)} copy(f32[2,256,2048]{2,1,0:T(8,128)} %constant_dynamic-update-slice_fusion) | data formatting | bytes 8388608 | tf_op jit(solution)/shard_map/reshape | solution.py:110
  197.6 1.0 constant_dynamic-slice_fusion.1
  198.7 1.4 fusion.49
  200.2 4.7 %convolution_subtract_fusion.1 = f32[192,2048]{1,0:T(8,128)S(1)} fusion(f32[192,512]{1,0:T(8,128)S(1)} %fusion.48, f32[512,2048]{1,0:T(8,128)} %bitcast.129, f32[192,1024]{1,0:T(8,128)S(1)} %bitcast.131, pred[]{:T(512)S(6)} %eq.94), kind=kOutput, calls=%fused_computation.8 | convolution fusion | flops 2416705536 | bytes 6946817 | tf_op jit(solution)/shard_map/dot_general | solution.py:18
  205.8 39.8 %all-reduce.7.cloned.1.call-done = f32[512,256]{1,0:T(8,128)} async-done(((f32[512,256]{1,0:T(8,128)}), f32[512,256]{1,0:T(8,128)}) %all-reduce.7.cloned.1.call-update) | async-done | bytes 524304 | tf_op jit(solution)/shard_map/psum | solution.py:137
  245.6 1.8 multiply_add_fusion
  247.5 1.5 constant_dynamic-slice_fusion.3
  250.0 1.5 collective-permute-start.3
  251.5 1.6 add_dynamic-update-slice_fusion
  254.5 1.5 collective-permute-start.8
  257.0 1.4 copy.23
  258.4 51.7 %collective-permute-done.6 = f32[8,64,256]{2,1,0:T(8,128)} collective-permute-done((f32[8,64,256]{2,1,0:T(8,128)}, f32[8,64,256]{2,1,0:T(8,128)}, u32[]{:S(2)}, u32[]{:S(2)}) %collective-permute-start.6) | collective-permute-done | bytes 524320 | tf_op jit(solution)/shard_map/ppermute | solution.py:14
  310.1 1.1 dynamic-slice_add_fusion.2
  311.1 9.7 %collective-permute-done.8 = f32[512,256]{1,0:T(8,128)} collective-permute-done((f32[512,256]{1,0:T(8,128)}, f32[512,256]{1,0:T(8,128)}, u32[]{:S(2)}, u32[]{:S(2)}) %collective-permute-start.8) | collective-permute-done | bytes 524320 | tf_op jit(solution)/shard_map/ppermute | solution.py:14
  320.9 2.2 convolution_negate_fusion
  323.8 1.4 convolution_bitcast_fusion
  325.3 43.1 %all-reduce.9.cloned.1.call-done = f32[256,256]{1,0:T(8,128)} async-done(((f32[256,256]{1,0:T(8,128)}), f32[256,256]{1,0:T(8,128)}) %all-reduce.9.cloned.1.call-update) | async-done | bytes 262160 | tf_op jit(solution)/shard_map/psum | solution.py:154
  368.4 2.5 dynamic-slice_add_fusion
  370.9 1.0 constant_dynamic-slice_fusion.2
  372.5 1.5 fusion.18
  375.1 2.3 dynamic-slice_add_fusion.1
  (119 shorter events, 24.9 us)
Async XLA Ops:
  7.2 1.2 copy-start
  7.2 105.2 %all-gather.5.cloned.1.call-start = ((), (), s32[]{:S(2)}) async-start(), calls=%async_computation | async-start | bytes 1310720 | tf_op jit(solution)/shard_map/all_gather | solution.py:28
  10.3 2.6 collective-permute-start
  26.8 23.8 %copy-start.8 = (f32[3,64,768]{2,1,0:T(8,128)S(1)}, f32[3,64,768]{2,1,0:T(8,128)}, u32[]{:S(2)}) copy-start(f32[3,64,768]{2,1,0:T(8,128)} %slice.137) | copy-start | bytes 1769476
  50.2 1.6 copy-start.5
  58.3 37.3 %copy-start.4 = (f32[3,64,1536]{2,1,0:T(8,128)}, f32[3,64,1536]{2,1,0:T(8,128)S(1)}, u32[]{:S(2)}) copy-start(f32[3,64,1536]{2,1,0:T(8,128)S(1)} %broadcast_select_fusion) | copy-start | bytes 3538948
  59.0 2.4 collective-permute-start.1
  62.4 19.9 %collective-permute-start.2 = (f32[2,64,1536]{2,1,0:T(8,128)}, f32[2,64,1536]{2,1,0:T(8,128)}, u32[]{:S(2)}, u32[]{:S(2)}) collective-permute-start(f32[2,64,1536]{2,1,0:T(8,128)} %fusion.90), channel_id=1, source_target_pairs={{0,8},{4,12},{8,0},{12,4},{16,24},{20,28},{24,16},{28,20},{1,9},{5... | collective-permute-start | bytes 2359304 | tf_op jit(solution)/shard_map/ppermute | solution.py:14
  83.8 0.9 copy-start.7
  83.8 4.5 %copy-start.9 = (f32[2,64,256]{2,1,0:T(8,128)S(1)}, f32[2,64,256]{2,1,0:T(8,128)}, u32[]{:S(2)}) copy-start(f32[2,64,256]{2,1,0:T(8,128)} %param.7) | copy-start | bytes 393220
  85.5 64.0 %all-gather.7.cloned.1.call-start = ((), (), s32[]{:S(2)}) async-start(), calls=%async_computation.1 | async-start | bytes 2621440 | tf_op jit(solution)/shard_map/all_gather | solution.py:103
  87.5 99.7 %all-gather.9.cloned.1.call-start = ((), (), s32[]{:S(2)}) async-start(), calls=%async_computation.2 | async-start | bytes 2621440 | tf_op jit(solution)/shard_map/all_gather | solution.py:104
  89.0 162.5 %collective-permute-start.5 = (f32[8,64,256]{2,1,0:T(8,128)}, f32[8,64,256]{2,1,0:T(8,128)}, u32[]{:S(2)}, u32[]{:S(2)}) collective-permute-start(f32[8,64,256]{2,1,0:T(8,128)} %constant_dynamic-update-slice_fusion.2), channel_id=1, source_target_pairs={{0,4},{4,0},{8,12},{12,8},{16,20},{20,16},{24,28},{28,24},{1,5},{5... | collective-permute-start | bytes 1572872 | tf_op jit(solution)/shard_map/ppermute | solution.py:14
  95.3 150.4 %all-reduce.7.cloned.1.call-start = ((), (), s32[]{:S(2)}) async-start(), calls=%async_computation.3 | async-start | bytes 1048576 | tf_op jit(solution)/shard_map/psum | solution.py:137
  115.1 4.9 %copy-start.2 = (f32[2,256,512]{2,1,0:T(8,128)S(1)}, f32[2,256,512]{2,1,0:T(8,128)}, u32[]{:S(2)}) copy-start(f32[2,256,512]{2,1,0:T(8,128)} %all-gather.5.cloned.1.call-done) | copy-start | bytes 3145732
  129.5 1.9 slice-start
  197.6 2.6 slice-start.1
  200.1 168.3 %all-reduce.9.cloned.1.call-start = ((), (), s32[]{:S(2)}) async-start(), calls=%async_computation.4 | async-start | bytes 524288 | tf_op jit(solution)/shard_map/psum | solution.py:154
  245.6 8.0 %collective-permute-start.7 = (f32[512,256]{1,0:T(8,128)}, f32[512,256]{1,0:T(8,128)S(1)}, u32[]{:S(2)}, u32[]{:S(2)}) collective-permute-start(f32[512,256]{1,0:T(8,128)} %all-reduce.7.cloned.1.call-done), channel_id=1, source_target_pairs={{0,4},{4,0},{8,12},{12,8},{16,20},{20,16},{24,28},{28,24},{1,5},{5... | collective-permute-start | bytes 1572872 | tf_op jit(solution)/shard_map/ppermute | solution.py:14
  247.4 2.6 copy-start.3
  247.5 6.2 %copy-start.10 = (f32[512,256]{1,0:T(8,128)S(1)}, f32[512,256]{1,0:T(8,128)}, u32[]{:S(2)}) copy-start(f32[512,256]{1,0:T(8,128)} %all-reduce.7.cloned.1.call-done) | copy-start | bytes 1572868
  247.5 8.5 %copy-start.6 = (f32[256,768]{1,0:T(8,128)S(1)}, f32[256,768]{1,0:T(8,128)}, u32[]{:S(2)}) copy-start(f32[256,768]{1,0:T(8,128)} %copy-done.5) | copy-start | bytes 2359300
  250.0 118.4 %collective-permute-start.3 = (f32[4,64,2048]{2,1,0:T(8,128)}, f32[4,64,2048]{2,1,0:T(8,128)}, u32[]{:S(2)}, u32[]{:S(2)}) collective-permute-start(f32[4,64,2048]{2,1,0:T(8,128)} %constant_dynamic-slice_fusion.3), channel_id=1, source_target_pairs={{0,8},{4,12},{8,0},{12,4},{16,24},{20,28},{24,16},{28,20},{1,9},{5... | collective-permute-start | bytes 6291464 | tf_op jit(solution)/shard_map/ppermute | solution.py:14
  253.1 57.0 %collective-permute-start.6 = (f32[8,64,256]{2,1,0:T(8,128)}, f32[8,64,256]{2,1,0:T(8,128)}, u32[]{:S(2)}, u32[]{:S(2)}) collective-permute-start(f32[8,64,256]{2,1,0:T(8,128)} %add_dynamic-update-slice_fusion), channel_id=1, source_target_pairs={{0,8},{4,12},{8,0},{12,4},{16,24},{20,28},{24,16},{28,20},{1,9},{5... | collective-permute-start | bytes 1572872 | tf_op jit(solution)/shard_map/ppermute | solution.py:14
  254.5 66.3 %collective-permute-start.8 = (f32[512,256]{1,0:T(8,128)}, f32[512,256]{1,0:T(8,128)}, u32[]{:S(2)}, u32[]{:S(2)}) collective-permute-start(f32[512,256]{1,0:T(8,128)} %add.281), channel_id=1, source_target_pairs={{0,8},{4,12},{8,0},{12,4},{16,24},{20,28},{24,16},{28,20},{1,9},{5... | collective-permute-start | bytes 1572872 | tf_op jit(solution)/shard_map/ppermute | solution.py:14
  368.4 4.1 %collective-permute-start.9 = (f32[256,256]{1,0:T(8,128)}, f32[256,256]{1,0:T(8,128)}, u32[]{:S(2)}, u32[]{:S(2)}) collective-permute-start(f32[256,256]{1,0:T(8,128)} %all-reduce.9.cloned.1.call-done), channel_id=1, source_target_pairs={{0,4},{4,0},{8,12},{12,8},{16,20},{20,16},{24,28},{28,24},{1,5},{5... | collective-permute-start | bytes 786440 | tf_op jit(solution)/shard_map/ppermute | solution.py:14
  371.9 3.1 collective-permute-start.4
  372.5 4.9 %copy-start.1 = (f32[4,64,1024]{2,1,0:T(8,128)S(1)}, f32[4,64,1024]{2,1,0:T(8,128)}, u32[]{:S(2)}) copy-start(f32[4,64,1024]{2,1,0:T(8,128)} %param.4) | copy-start | bytes 3145732
Sparse Core Ops, SparseCore 0:
  85.6 26.7 all-gather.4
  114.3 35.1 all-gather.6
  151.9 35.1 all-gather.8
  200.2 45.3 all-reduce.6
  325.3 43.0 all-reduce.8
where the time goes:
time: 385 us; the launch traced here: 384 us
  waiting for transfers between devices  234 us (61%)
  local copies, waits for them, and re-layouts  38.4 us (10%)
  matrix products  32.8 us (9%)
  blocking collectives  32.7 us (8%)
  other arithmetic  19.8 us (5%)
  between operations  19.8 us (5%)
  starting transfers between devices  6.62 us (2%)
    ppermute x10, waiting for transfers between devices, swapped(): return lax.ppermute(value, axis, pairs)  82.2 us
    psum x1, waiting for transfers between devices, shards(): partial_one = lax.psum(partial_one, 'sub')  43.1 us
    psum x1, waiting for transfers between devices, shards(): partial_two = lax.psum(partial_two, 'sub')  39.8 us
    all_gather x1, waiting for transfers between devices, shards(): lax.all_gather(second_node[:, :, :4 * W], 'sub', axis=1, tiled=True)  34.4 us
    dot_general x24, matrix products, exact_dot(): jnp.dot(left_matrix, right_matrix, precision=lax.Precision.HIGHEST, prefe...  32.8 us
    all_gather x1, waiting for transfers between devices, shards(): lax.all_gather(first_node[:, :, :4 * W], 'sub', axis=1, tiled=True)  17.2 us
    all_gather x1, waiting for transfers between devices, interface_inverse(): lax.all_gather(block_rows, 'sub', axis=1, tiled=True)  16.9 us
    all_gather x1, blocking collectives, shards(): lax.all_gather(second_piece[:, :3 * W], 'sub', axis=0, tiled=True)  12.5 us
  transfers between devices with their start and end apart: 15, of which 10 were waited for; matrix products, arithmetic and copies ran while one was open for 18% of the time, Pallas kernels for 0%

commit v1 on v0

--- a/solution.py
+++ b/solution.py
@@ -2,10 +2,38 @@
 import jax.numpy as jnp
 from jax import lax
 from jax.sharding import PartitionSpec as P
+from jax.lax import axis_index, ppermute, psum
 
 W = 256
 K = 256
 NS_STEPS = 4
+
+
+def check_task(tile_in, dim_at):
+    now, parts_out, mixed_arr = (psum(1, "sub"), axis_index("sub"), tile_in.shape[dim_at])
+    xs_all = []
+    for dd in range(now):
+        xs_all.append((dd, (dd + 1) % now))
+    log = []
+    for dd in range(now):
+        log.append((dd, (dd - 1) % now))
+    y2 = jnp.zeros(
+        (*tile_in.shape[:dim_at], now * mixed_arr, *tile_in.shape[dim_at + 1 :]), tile_in.dtype
+    )
+    y2 = lax.dynamic_update_slice_in_dim(y2, tile_in, parts_out * mixed_arr, axis=dim_at)
+    current_value = front = tile_in
+    v_now = now // 2
+    for k in range(1, v_now + 1):
+        current_value = ppermute(current_value, "sub", xs_all)
+        y2 = lax.dynamic_update_slice_in_dim(
+            y2, current_value, (parts_out - k) % now * mixed_arr, axis=dim_at
+        )
+        if k < now - v_now:
+            front = ppermute(front, "sub", log)
+            y2 = lax.dynamic_update_slice_in_dim(
+                y2, front, (parts_out + k) % now * mixed_arr, axis=dim_at
+            )
+    return y2
 
 
 def swapped(value, axis, apart):
@@ -25,9 +53,7 @@
 
 def interface_inverse(block_rows):
     slot_count, width_local, block_size = block_rows.shape
-    full_block = lax.all_gather(block_rows, "sub", axis=1, tiled=True).reshape(
-        block_size, block_size
-    )
+    full_block = check_task(block_rows, 1).reshape(block_size, block_size)
     row_bound = jnp.max(jnp.sum(jnp.abs(full_block), axis=1))
     iterate = jnp.eye(block_size, dtype=jnp.float32) / row_bound
     for iteration in range(NS_STEPS):

time: 385 us -> 364 us (0.945)
  waiting for transfers between devices: 234 us -> 211 us
  starting transfers between devices: 6.62 us -> 15.7 us
  blocking collectives: 32.7 us -> 23.9 us
    ppermute x0 -> x6, waiting for transfers between devices: none -> 18.2 us  [the longest x4 13.6 us: check_task(): current_value = ppermute(current_value, 'sub', xs_all)]
    all_gather x1, waiting for transfers between devices: 17.2 us -> 0.02 us  [shards(): lax.all_gather(first_node[:, :, :4 * W], 'sub', axis=1, tiled=True)]
    all_gather x1 -> x0, waiting for transfers between devices: 16.9 us -> none  [interface_inverse(): lax.all_gather(block_rows, 'sub', axis=1, tiled=True)]
    all_gather x1 -> x0, blocking collectives: 10 us -> none  [interface_inverse(): lax.all_gather(block_rows, 'sub', axis=1, tiled=True)]
    ppermute x0 -> x6, starting transfers between devices: none -> 9.11 us  [the longest x2 5.72 us: check_task(): front = ppermute(front, 'sub', log)]
    all_gather x1, waiting for transfers between devices: 34.4 us -> 27.6 us  [shards(): lax.all_gather(second_node[:, :, :4 * W], 'sub', axis=1, tiled=True)]
  transfers between devices with their start and end apart: 15 -> 20, of which waited for: 10 -> 12; matrix products, arithmetic and copies ran while one was open for 18% -> 19% of each run, Pallas kernels for 0% -> 0%
where the time goes in v1:
time: 364 us; the launch traced here: 363 us
  waiting for transfers between devices  211 us (58%)
  local copies, waits for them, and re-layouts  40.9 us (11%)
  matrix products  31.5 us (9%)
  blocking collectives  23.9 us (7%)
  other arithmetic  20.5 us (6%)
  between operations  19.5 us (5%)
  starting transfers between devices  15.7 us (4%)
    ppermute x10, waiting for transfers between devices, swapped(): return lax.ppermute(value, axis, pairs)  82.2 us
    psum x1, waiting for transfers between devices, shards(): partial_one = lax.psum(partial_one, 'sub')  43.1 us
    psum x1, waiting for transfers between devices, shards(): partial_two = lax.psum(partial_two, 'sub')  39.9 us
    dot_general x24, matrix products, exact_dot(): jnp.dot(left_matrix, right_matrix, precision=lax.Precision.HIGHEST, prefe...  31.5 us
    all_gather x1, waiting for transfers between devices, shards(): lax.all_gather(second_node[:, :, :4 * W], 'sub', axis=1, tiled=True)  27.6 us
    ppermute x4, waiting for transfers between devices, check_task(): current_value = ppermute(current_value, 'sub', xs_all)  13.6 us
    all_gather x1, blocking collectives, shards(): lax.all_gather(second_piece[:, :3 * W], 'sub', axis=0, tiled=True)  12.2 us
    all_gather x1, blocking collectives, shards(): lax.all_gather(first_piece[:, :3 * W], 'sub', axis=0, tiled=True)  11.7 us
  transfers between devices with their start and end apart: 20, of which 12 were waited for; matrix products, arithmetic and copies ran while one was open for 19% of the time, Pallas kernels for 0%

profile of v1, /device:TPU:0, one launch (start us, length us, event | category | flops | bytes accessed | tf_op | source)
XLA Modules:
  0.0 363.1 jit_solution(9465776020700835497)
XLA Ops:
  13.1 3.5 collective-permute-start.2
  16.7 12.2 %all_gather.13 = f32[256,768]{1,0:T(8,128)S(1)} all-gather(f32[64,768]{1,0:T(8,128)S(1)} %slice.143), channel_id=1, replica_groups=mesh['leaf'=8,'sub'=4] {'sub'}, dimensions={0}, use_global_device_ids=true | all-gather | bytes 983040 | tf_op jit(solution)/shard_map/all_gather | solution.py:86
  28.9 11.7 %all_gather.12 = f32[256,768]{1,0:T(8,128)S(1)} all-gather(f32[64,768]{1,0:T(8,128)S(1)} %slice.142), channel_id=1, replica_groups=mesh['leaf'=8,'sub'=4] {'sub'}, dimensions={0}, use_global_device_ids=true | all-gather | bytes 983040 | tf_op jit(solution)/shard_map/all_gather | solution.py:85
  40.5 1.7 collective-permute-start.3
  42.3 3.4 collective-permute-done.3
  50.6 1.2 convolution_subtract_fusion
  51.9 1.5 reshape_reshape.3
  53.4 2.8 copy.22
  56.2 1.9 gather_fusion.3
  59.2 2.3 collective-permute-done.4
  62.5 1.6 collective-permute-start.5
  64.1 18.3 %collective-permute-done.5 = f32[2,64,1536]{2,1,0:T(8,128)} collective-permute-done((f32[2,64,1536]{2,1,0:T(8,128)}, f32[2,64,1536]{2,1,0:T(8,128)}, u32[]{:S(2)}, u32[]{:S(2)}) %collective-permute-start.5) | collective-permute-done | bytes 786464 | tf_op jit(solution)/shard_map/ppermute | solution.py:42
  82.4 2.4 broadcast_select_fusion.3
  88.1 1.8 constant_dynamic-update-slice_fusion.4
  93.9 2.2 collective-permute-start.7
  97.2 5.8 %collective-permute-done.6 = f32[2,64,512]{2,1,0:T(8,128)} collective-permute-done((f32[2,64,512]{2,1,0:T(8,128)}, f32[2,64,512]{2,1,0:T(8,128)}, u32[]{:S(2)}, u32[]{:S(2)}) %collective-permute-start.6) | collective-permute-done | bytes 262176 | tf_op jit(solution)/shard_map/ppermute | solution.py:27
  103.9 1.1 copy-done.6
  107.1 4.6 %collective-permute-done.7 = f32[2,64,512]{2,1,0:T(8,128)} collective-permute-done((f32[2,64,512]{2,1,0:T(8,128)}, f32[2,64,512]{2,1,0:T(8,128)}, u32[]{:S(2)}, u32[]{:S(2)}) %collective-permute-start.7) | collective-permute-done | bytes 262176 | tf_op jit(solution)/shard_map/ppermute | solution.py:32
  112.7 4.3 %collective-permute-done.8 = f32[2,64,512]{2,1,0:T(8,128)} collective-permute-done((f32[2,64,512]{2,1,0:T(8,128)}, f32[2,64,512]{2,1,0:T(8,128)}, u32[]{:S(2)}, u32[]{:S(2)}) %collective-permute-start.8) | collective-permute-done | bytes 262176 | tf_op jit(solution)/shard_map/ppermute | solution.py:27
  119.5 1.8 fusion.2
  121.3 1.8 fusion.7
  123.0 1.8 fusion.47
  124.9 1.8 convolution_subtract_fusion.4
  126.8 1.8 fusion.48
  128.6 1.8 convolution_subtract_fusion.3
  130.5 2.1 fusion.49
  132.6 1.9 convolution_subtract_fusion.2
  135.3 3.3 constant_dynamic-update-slice_fusion.6
  138.6 27.6 %all-gather.5.cloned.1.call-done = f32[2,256,1024]{2,1,0:T(8,128)} async-done(((f32[2,64,1024]{2,1,0:T(8,128)}), f32[2,256,1024]{2,1,0:T(8,128)}) %all-gather.5.cloned.1.call-update) | async-done | bytes 2097168 | tf_op jit(solution)/shard_map/all_gather | solution.py:130
  166.2 3.3 constant_dynamic-update-slice_fusion.5
  169.5 7.3 %copy.26 = f32[2,256,2048]{1,0,2:T(2,128)} copy(f32[2,256,2048]{2,1,0:T(8,128)} %constant_dynamic-update-slice_fusion.5) | data formatting | bytes 8388608 | tf_op jit(solution)/shard_map/reshape | solution.py:136
  177.9 1.4 fusion.51
  179.4 4.7 %convolution_subtract_fusion.1 = f32[192,2048]{1,0:T(8,128)S(1)} fusion(f32[192,512]{1,0:T(8,128)S(1)} %fusion.50, f32[512,2048]{1,0:T(8,128)} %bitcast.137, f32[192,1024]{1,0:T(8,128)S(1)} %bitcast.139, pred[]{:T(512)S(6)} %eq.100), kind=kOutput, calls=%fused_computation.8 | convolution fusion | flops 2416705536 | bytes 6946817 | tf_op jit(solution)/shard_map/dot_general | solution.py:46
  185.0 39.9 %all-reduce.7.cloned.1.call-done = f32[512,256]{1,0:T(8,128)} async-done(((f32[512,256]{1,0:T(8,128)}), f32[512,256]{1,0:T(8,128)}) %all-reduce.7.cloned.1.call-update) | async-done | bytes 524304 | tf_op jit(solution)/shard_map/psum | solution.py:163
  224.9 1.8 multiply_add_fusion
  226.7 1.5 constant_dynamic-slice_fusion.3
  229.3 1.5 collective-permute-start.9
  230.8 1.6 add_dynamic-update-slice_fusion
  233.8 1.5 collective-permute-start.14
  236.2 1.4 copy.25
  237.6 51.7 %collective-permute-done.12 = f32[8,64,256]{2,1,0:T(8,128)} collective-permute-done((f32[8,64,256]{2,1,0:T(8,128)}, f32[8,64,256]{2,1,0:T(8,128)}, u32[]{:S(2)}, u32[]{:S(2)}) %collective-permute-start.12) | collective-permute-done | bytes 524320 | tf_op jit(solution)/shard_map/ppermute | solution.py:42
  290.4 9.7 %collective-permute-done.14 = f32[512,256]{1,0:T(8,128)} collective-permute-done((f32[512,256]{1,0:T(8,128)}, f32[512,256]{1,0:T(8,128)}, u32[]{:S(2)}, u32[]{:S(2)}) %collective-permute-start.14) | collective-permute-done | bytes 524320 | tf_op jit(solution)/shard_map/ppermute | solution.py:42
  300.1 2.2 convolution_negate_fusion
  303.0 1.4 convolution_bitcast_fusion
  304.5 43.1 %all-reduce.9.cloned.1.call-done = f32[256,256]{1,0:T(8,128)} async-done(((f32[256,256]{1,0:T(8,128)}), f32[256,256]{1,0:T(8,128)}) %all-reduce.9.cloned.1.call-update) | async-done | bytes 262160 | tf_op jit(solution)/shard_map/psum | solution.py:180
  347.6 2.5 dynamic-slice_add_fusion
  351.7 1.5 fusion.18
  354.3 2.3 dynamic-slice_add_fusion.1
  (135 shorter events, 33.2 us)
Async XLA Ops:
  7.2 1.2 copy-start
  7.2 128.2 %all-gather.3.cloned.1.call-start = ((), (), s32[]{:S(2)}) async-start(), calls=%async_computation | async-start | bytes 2621440 | tf_op jit(solution)/shard_map/all_gather | solution.py:129
  10.3 2.7 collective-permute-start
  13.1 29.1 %collective-permute-start.2 = (f32[1,64,256]{2,1,0:T(8,128)S(1)}, f32[1,64,256]{2,1,0:T(8,128)S(1)}, u32[]{:S(2)}, u32[]{:S(2)}) collective-permute-start(f32[1,64,256]{2,1,0:T(8,128)S(1)} %get-tuple-element.13), channel_id=1, source_target_pairs={{0,3},{1,0},{2,1},{3,2},{4,7},{5,4},{6,5},{7,6},{8,11},{9,8},{10,9... | collective-permute-start | bytes 196616 | tf_op jit(solution)/shard_map/ppermute | solution.py:32
  16.6 23.9 %collective-permute-start.1 = (f32[1,64,256]{2,1,0:T(8,128)S(1)}, f32[1,64,256]{2,1,0:T(8,128)S(1)}, u32[]{:S(2)}, u32[]{:S(2)}) collective-permute-start(f32[1,64,256]{2,1,0:T(8,128)S(1)} %get-tuple-element.13), channel_id=1, source_target_pairs={{0,1},{1,2},{2,3},{3,0},{4,5},{5,6},{6,7},{7,4},{8,9},{9,10},{10,1... | collective-permute-start | bytes 196616 | tf_op jit(solution)/shard_map/ppermute | solution.py:27
  40.5 10.1 %copy-start.4 = (f32[256,768]{1,0:T(8,128)}, f32[256,768]{1,0:T(8,128)S(1)}, u32[]{:S(2)}) copy-start(f32[256,768]{1,0:T(8,128)S(1)} %all_gather.12) | copy-start | bytes 2359300
  40.5 5.2 %collective-permute-start.3 = (f32[1,64,256]{2,1,0:T(8,128)S(1)}, f32[1,64,256]{2,1,0:T(8,128)S(1)}, u32[]{:S(2)}, u32[]{:S(2)}) collective-permute-start(f32[1,64,256]{2,1,0:T(8,128)S(1)} %collective-permute-done.1), channel_id=1, source_target_pairs={{0,1},{1,2},{2,3},{3,0},{4,5},{5,6},{6,7},{7,4},{8,9},{9,10},{10,1... | collective-permute-start | bytes 196616 | tf_op jit(solution)/shard_map/ppermute | solution.py:27
  48.7 1.9 copy-start.8
  58.3 45.6 %copy-start.3 = (f32[3,64,1536]{2,1,0:T(8,128)}, f32[3,64,1536]{2,1,0:T(8,128)S(1)}, u32[]{:S(2)}) copy-start(f32[3,64,1536]{2,1,0:T(8,128)S(1)} %broadcast_select_fusion) | copy-start | bytes 3538948
  59.1 2.4 collective-permute-start.4
  62.5 19.9 %collective-permute-start.5 = (f32[2,64,1536]{2,1,0:T(8,128)}, f32[2,64,1536]{2,1,0:T(8,128)}, u32[]{:S(2)}, u32[]{:S(2)}) collective-permute-start(f32[2,64,1536]{2,1,0:T(8,128)} %fusion.92), channel_id=1, source_target_pairs={{0,8},{4,12},{8,0},{12,4},{16,24},{20,28},{24,16},{28,20},{1,9},{5... | collective-permute-start | bytes 2359304 | tf_op jit(solution)/shard_map/ppermute | solution.py:42
  64.1 22.5 %copy-start.9 = (f32[2,64,256]{2,1,0:T(8,128)S(1)}, f32[2,64,256]{2,1,0:T(8,128)}, u32[]{:S(2)}) copy-start(f32[2,64,256]{2,1,0:T(8,128)} %param.7) | copy-start | bytes 393220
  84.7 2.5 copy-start.7
  85.7 80.6 %all-gather.5.cloned.1.call-start = ((), (), s32[]{:S(2)}) async-start(), calls=%async_computation.1 | async-start | bytes 2621440 | tf_op jit(solution)/shard_map/all_gather | solution.py:130
  87.2 143.5 %collective-permute-start.11 = (f32[8,64,256]{2,1,0:T(8,128)}, f32[8,64,256]{2,1,0:T(8,128)}, u32[]{:S(2)}, u32[]{:S(2)}) collective-permute-start(f32[8,64,256]{2,1,0:T(8,128)} %constant_dynamic-update-slice_fusion), channel_id=1, source_target_pairs={{0,4},{4,0},{8,12},{12,8},{16,20},{20,16},{24,28},{28,24},{1,5},{5... | collective-permute-start | bytes 1572872 | tf_op jit(solution)/shard_map/ppermute | solution.py:42
  89.9 13.1 %collective-permute-start.6 = (f32[2,64,512]{2,1,0:T(8,128)}, f32[2,64,512]{2,1,0:T(8,128)}, u32[]{:S(2)}, u32[]{:S(2)}) collective-permute-start(f32[2,64,512]{2,1,0:T(8,128)} %get-tuple-element.5), channel_id=1, source_target_pairs={{0,1},{1,2},{2,3},{3,0},{4,5},{5,6},{6,7},{7,4},{8,9},{9,10},{10,1... | collective-permute-start | bytes 786440 | tf_op jit(solution)/shard_map/ppermute | solution.py:27
  93.9 17.9 %collective-permute-start.7 = (f32[2,64,512]{2,1,0:T(8,128)}, f32[2,64,512]{2,1,0:T(8,128)}, u32[]{:S(2)}, u32[]{:S(2)}) collective-permute-start(f32[2,64,512]{2,1,0:T(8,128)} %get-tuple-element.5), channel_id=1, source_target_pairs={{0,3},{1,0},{2,1},{3,2},{4,7},{5,4},{6,5},{7,6},{8,11},{9,8},{10,9... | collective-permute-start | bytes 786440 | tf_op jit(solution)/shard_map/ppermute | solution.py:32
  103.0 14.0 %collective-permute-start.8 = (f32[2,64,512]{2,1,0:T(8,128)}, f32[2,64,512]{2,1,0:T(8,128)}, u32[]{:S(2)}, u32[]{:S(2)}) collective-permute-start(f32[2,64,512]{2,1,0:T(8,128)} %collective-permute-done.6), channel_id=1, source_target_pairs={{0,1},{1,2},{2,3},{3,0},{4,5},{5,6},{6,7},{7,4},{8,9},{9,10},{10,1... | collective-permute-start | bytes 786440 | tf_op jit(solution)/shard_map/ppermute | solution.py:27
  103.9 1.1 copy-start.6
  105.9 118.9 %all-reduce.7.cloned.1.call-start = ((), (), s32[]{:S(2)}) async-start(), calls=%async_computation.2 | async-start | bytes 1048576 | tf_op jit(solution)/shard_map/psum | solution.py:163
  132.6 1.9 slice-start
  176.8 2.6 slice-start.1
  179.3 168.3 %all-reduce.9.cloned.1.call-start = ((), (), s32[]{:S(2)}) async-start(), calls=%async_computation.3 | async-start | bytes 524288 | tf_op jit(solution)/shard_map/psum | solution.py:180
  224.9 8.0 %collective-permute-start.13 = (f32[512,256]{1,0:T(8,128)}, f32[512,256]{1,0:T(8,128)S(1)}, u32[]{:S(2)}, u32[]{:S(2)}) collective-permute-start(f32[512,256]{1,0:T(8,128)} %all-reduce.7.cloned.1.call-done), channel_id=1, source_target_pairs={{0,4},{4,0},{8,12},{12,8},{16,20},{20,16},{24,28},{28,24},{1,5},{5... | collective-permute-start | bytes 1572872 | tf_op jit(solution)/shard_map/ppermute | solution.py:42
  226.7 2.6 copy-start.2
  226.7 6.2 %copy-start.10 = (f32[512,256]{1,0:T(8,128)S(1)}, f32[512,256]{1,0:T(8,128)}, u32[]{:S(2)}) copy-start(f32[512,256]{1,0:T(8,128)} %all-reduce.7.cloned.1.call-done) | copy-start | bytes 1572868
  226.7 8.6 %copy-start.5 = (f32[256,768]{1,0:T(8,128)S(1)}, f32[256,768]{1,0:T(8,128)}, u32[]{:S(2)}) copy-start(f32[256,768]{1,0:T(8,128)} %copy-done.4) | copy-start | bytes 2359300
  229.3 118.4 %collective-permute-start.9 = (f32[4,64,2048]{2,1,0:T(8,128)}, f32[4,64,2048]{2,1,0:T(8,128)}, u32[]{:S(2)}, u32[]{:S(2)}) collective-permute-start(f32[4,64,2048]{2,1,0:T(8,128)} %constant_dynamic-slice_fusion.3), channel_id=1, source_target_pairs={{0,8},{4,12},{8,0},{12,4},{16,24},{20,28},{24,16},{28,20},{1,9},{5... | collective-permute-start | bytes 6291464 | tf_op jit(solution)/shard_map/ppermute | solution.py:42
  232.3 57.0 %collective-permute-start.12 = (f32[8,64,256]{2,1,0:T(8,128)}, f32[8,64,256]{2,1,0:T(8,128)}, u32[]{:S(2)}, u32[]{:S(2)}) collective-permute-start(f32[8,64,256]{2,1,0:T(8,128)} %add_dynamic-update-slice_fusion), channel_id=1, source_target_pairs={{0,8},{4,12},{8,0},{12,4},{16,24},{20,28},{24,16},{28,20},{1,9},{5... | collective-permute-start | bytes 1572872 | tf_op jit(solution)/shard_map/ppermute | solution.py:42
  233.8 66.3 %collective-permute-start.14 = (f32[512,256]{1,0:T(8,128)}, f32[512,256]{1,0:T(8,128)}, u32[]{:S(2)}, u32[]{:S(2)}) collective-permute-start(f32[512,256]{1,0:T(8,128)} %add.320), channel_id=1, source_target_pairs={{0,8},{4,12},{8,0},{12,4},{16,24},{20,28},{24,16},{28,20},{1,9},{5... | collective-permute-start | bytes 1572872 | tf_op jit(solution)/shard_map/ppermute | solution.py:42
  347.6 4.1 %collective-permute-start.15 = (f32[256,256]{1,0:T(8,128)}, f32[256,256]{1,0:T(8,128)}, u32[]{:S(2)}, u32[]{:S(2)}) collective-permute-start(f32[256,256]{1,0:T(8,128)} %all-reduce.9.cloned.1.call-done), channel_id=1, source_target_pairs={{0,4},{4,0},{8,12},{12,8},{16,20},{20,16},{24,28},{28,24},{1,5},{5... | collective-permute-start | bytes 786440 | tf_op jit(solution)/shard_map/ppermute | solution.py:42
  351.2 3.1 collective-permute-start.10
  351.7 4.9 %copy-start.1 = (f32[4,64,1024]{2,1,0:T(8,128)S(1)}, f32[4,64,1024]{2,1,0:T(8,128)}, u32[]{:S(2)}) copy-start(f32[4,64,1024]{2,1,0:T(8,128)} %param.4) | copy-start | bytes 3145732
Sparse Core Ops, SparseCore 0:
  85.8 42.4 all-gather.2
  130.7 35.4 all-gather.4
  179.4 45.3 all-reduce.6
  304.5 43.0 all-reduce.8
